TPU v7x, 32 devices: a whole 2x2x4 slice. The times are simulated.
32 devices in a mesh: prow: 8 (over z, y), pcol: 4 (over x, core).
Axes of the slice: x: 2, y: 2, z: 4, core: 2. Of those that a mesh axis runs over, the one named last changes fastest.
Arguments:
- a_panel: float32 [98304, 512], P('prow', 'pcol'), may hold values from -6 to 6
- u_rows: float32 [512, 98304], P('pcol', 'prow'), may hold values from -0.25 to 0.25
- u_col: float32 [98304, 2048], P('prow', 'pcol'), may hold values from -0.01953125 to 0.01953125
- c_in: float32 [98304, 2048], P('prow', 'pcol'), may hold values from -6 to 6
Outputs:
- c_out: float32 [98304, 2048], P('prow', 'pcol')
All inputs are finite; a program needn't handle non-finite values.
Results may differ from a plain program's by a relative error of at most 0.00007.
Values sent between devices are 32-bit elements; how exact they have to be, the bound alone decides.
A program may use at most 192 MiB of HBM per device.

v0:
```python
import jax
import jax.numpy as jnp
from jax import lax
from jax.sharding import PartitionSpec as P


def gather_later(u_rows):
    return lax.all_gather(u_rows, "pcol", axis=0, tiled=True)


def on_device(a_panel, u_rows, u_col, c_in):
    a_full = lax.all_gather(a_panel, "pcol", axis=1, tiled=True)
    partial_inner = jnp.dot(
        a_full.T, u_col, precision=lax.Precision.HIGHEST, preferred_element_type=jnp.float32
    )
    inner = lax.psum(partial_inner, "prow")
    u_full = gather_later(u_rows)
    result = c_in + jnp.dot(
        u_full.T, inner, precision=lax.Precision.HIGHEST, preferred_element_type=jnp.float32
    )
    return result


def solution(mesh):
    placed = (P("prow", "pcol"), P("pcol", "prow"), P("prow", "pcol"), P("prow", "pcol"))
    return jax.shard_map(
        on_device, mesh=mesh, in_specs=placed, out_specs=P("prow", "pcol"), check_vma=False
    )
```

profile of v0, /device:TPU:0, one launch (start us, length us, event | category | flops | bytes accessed | tf_op | source)
XLA Modules:
  0.0 486.4 jit_solution(6694891880605975887)
XLA Ops:
  6.5 0.0 all-gather.3.cloned.1.call-start
  6.5 0.7 all-gather.3.cloned.1.call-update
  7.3 0.0 all-gather.5.cloned.1.call-start
  7.3 0.7 all-gather.5.cloned.1.call-update
  8.0 0.0 all-reduce.2.cloned.1.call-start
  8.1 161.7 %all-gather.3.cloned.1.call-done = f32[12288,512]{1,0:T(8,128)} async-done(((f32[12288,128]{1,0:T(8,128)}), f32[12288,512]{1,0:T(8,128)}) %all-gather.3.cloned.1.call-update) | async-done | bytes 25165840 | tf_op jit(solution)/shard_map/all_gather | solution.py:12
  169.8 45.2 %fusion = f32[512,512]{1,0:T(8,128)} fusion(f32[12288,512]{1,0:T(8,128)} %all-gather.3.cloned.1.call-done, f32[12288,512]{1,0:T(8,128)} %param.6), kind=kOutput, calls=%fused_computation.1 | convolution fusion | flops 38654705664 | bytes 51380224 | tf_op jit(solution)/shard_map/dot_general | solution.py:13
  215.0 0.0 all-reduce.2.cloned.1.call-update
  215.0 24.7 %copy.5 = f32[12288,512]{0,1:T(8,128)} copy(f32[12288,512]{1,0:T(8,128)} %param.7) | data formatting | bytes 50331648 | tf_op args[3]
  239.7 86.5 %all-gather.5.cloned.1.call-done = f32[512,12288]{1,0:T(8,128)} async-done(((f32[128,12288]{1,0:T(8,128)}), f32[512,12288]{1,0:T(8,128)}) %all-gather.5.cloned.1.call-update) | async-done | bytes 25165840 | tf_op jit(solution)/shard_map/all_gather | solution.py:8
  326.2 81.8 %all-reduce.2.cloned.1.call-done = f32[512,512]{1,0:T(8,128)} async-done(((f32[512,512]{1,0:T(8,128)}), f32[512,512]{1,0:T(8,128)}) %all-reduce.2.cloned.1.call-update) | async-done | bytes 1048592 | tf_op jit(solution)/shard_map/psum | solution.py:16
  407.9 47.2 %bitcast_add_fusion = f32[12288,512]{0,1:T(8,128)} fusion(f32[12288,512]{0,1:T(8,128)} %copy.5, f32[512,512]{1,0:T(8,128)} %all-reduce.2.cloned.1.call-done, f32[512,12288]{1,0:T(8,128)} %all-gather.5.cloned.1.call-done), kind=kOutput, calls=%fused_computation | convolution fusion | flops 38660997120 | bytes 76546048 | tf_op jit(solution)/shard_map/dot_general | solution.py:18
  455.2 24.7 %copy.6 = f32[12288,512]{1,0:T(8,128)} copy(f32[12288,512]{0,1:T(8,128)} %bitcast_add_fusion) | data formatting | bytes 50331648 | tf_op jit(solution)/shard_map/add | solution.py:18
Async XLA Ops:
  6.5 163.3 %all-gather.3.cloned.1.call-start = ((), (), s32[]{:S(2)}) async-start(), calls=%async_computation | async-start | bytes 31457280 | tf_op jit(solution)/shard_map/all_gather | solution.py:12
  7.3 318.9 %all-gather.5.cloned.1.call-start = ((), (), s32[]{:S(2)}) async-start(), calls=%async_computation.2 | async-start | bytes 31457280 | tf_op jit(solution)/shard_map/all_gather | solution.py:8
  8.0 399.9 %all-reduce.2.cloned.1.call-start = ((), (), s32[]{:S(2)}) async-start(), calls=%async_computation.1 | async-start | bytes 2097152 | tf_op jit(solution)/shard_map/psum | solution.py:16
Sparse Core Ops, SparseCore 0:
  8.9 160.8 all-gather.2
  171.4 154.7 all-gather.4
  329.7 78.1 all-reduce.1
where the time goes:
time: 487 us; the launch traced here: 486 us
  waiting for transfers between devices  331 us (68%)
  matrix products  92.4 us (19%)
  local copies, waits for them, and re-layouts  49.4 us (10%)
  between operations  13.1 us (3%)
    all_gather x1, waiting for transfers between devices, on_device(): a_full = lax.all_gather(a_panel, 'pcol', axis=1, tiled=True)  162 us
    all_gather x1, waiting for transfers between devices, gather_later(): return lax.all_gather(u_rows, 'pcol', axis=0, tiled=True)  86.5 us
    psum x1, waiting for transfers between devices, on_device(): inner = lax.psum(partial_inner, 'prow')  81.8 us
    dot_general x1, matrix products, on_device(): jnp.dot(u_full.T, inner, precision=lax.Precision.HIGHEST, preferred_eleme...  47.2 us
    dot_general x1, matrix products, on_device(): jnp.dot(a_full.T, u_col, precision=lax.Precision.HIGHEST, preferred_eleme...  45.2 us
    unnamed x1, local copies, waits for them, and re-layouts  24.7 us
    add x1, local copies, waits for them, and re-layouts, on_device(): c_in + jnp.dot(u_full.T, inner, precision=lax.Precision.HIGHEST, preferre...  24.7 us
  transfers between devices with their start and end apart: 3, of which 3 were waited for; matrix products, arithmetic and copies ran while one was open for 14% of the time, Pallas kernels for 0%

commit v1 on v0

--- a/solution.py
+++ b/solution.py
@@ -13,7 +13,12 @@
     partial_inner = jnp.dot(
         a_full.T, u_col, precision=lax.Precision.HIGHEST, preferred_element_type=jnp.float32
     )
-    inner = lax.psum(partial_inner, "prow")
+    shares = lax.axis_size("prow")
+    inner, y2 = (partial_inner, 0)
+    while 1 << y2 < shares:
+        found_now = lax.ppermute(inner, "prow", [(i0, i0 ^ 1 << y2) for i0 in range(shares)])
+        inner = inner + found_now
+        y2 = y2 + 1
     u_full = gather_later(u_rows)
     result = c_in + jnp.dot(
         u_full.T, inner, precision=lax.Precision.HIGHEST, preferred_element_type=jnp.float32

time: 487 us -> 406 us (0.83)
  waiting for transfers between devices: 331 us -> 245 us
  starting transfers between devices: 0.08 us -> 5.59 us
    psum x1 -> x0, waiting for transfers between devices: 81.8 us -> none  [on_device(): inner = lax.psum(partial_inner, 'prow')]
    all_gather x1, waiting for transfers between devices: 86.5 us -> 34.5 us  [gather_later(): return lax.all_gather(u_rows, 'pcol', axis=0, tiled=True)]
    ppermute x0 -> x3, waiting for transfers between devices: none -> 46.9 us  [on_device(): lax.ppermute(inner, 'prow', [(i0, i0 ^ 1 << y2) for i0 in range(shares)])]
    ppermute x0 -> x3, starting transfers between devices: none -> 5.55 us  [on_device(): lax.ppermute(inner, 'prow', [(i0, i0 ^ 1 << y2) for i0 in range(shares)])]
  transfers between devices with their start and end apart: 3 -> 5, of which waited for: 3 -> 4; matrix products, arithmetic and copies ran while one was open for 14% -> 17% of each run, Pallas kernels for 0% -> 0%
where the time goes in v1:
time: 406 us; the launch traced here: 405 us
  waiting for transfers between devices  245 us (60%)
  matrix products  91.5 us (23%)
  local copies, waits for them, and re-layouts  49.4 us (12%)
  between operations  13.4 us (3%)
  starting transfers between devices  5.59 us (1%)
    all_gather x1, waiting for transfers between devices, on_device(): a_full = lax.all_gather(a_panel, 'pcol', axis=1, tiled=True)  162 us
    dot_general x1, matrix products, on_device(): jnp.dot(u_full.T, inner, precision=lax.Precision.HIGHEST, preferred_eleme...  47.2 us
    ppermute x3, waiting for transfers between devices, on_device(): lax.ppermute(inner, 'prow', [(i0, i0 ^ 1 << y2) for i0 in range(shares)])  46.9 us
    dot_general x1, matrix products, on_device(): jnp.dot(a_full.T, u_col, precision=lax.Precision.HIGHEST, preferred_eleme...  44.3 us
    all_gather x1, waiting for transfers between devices, gather_later(): return lax.all_gather(u_rows, 'pcol', axis=0, tiled=True)  34.5 us
    unnamed x1, local copies, waits for them, and re-layouts  24.7 us
    add x1, local copies, waits for them, and re-layouts, on_device(): c_in + jnp.dot(u_full.T, inner, precision=lax.Precision.HIGHEST, preferre...  24.7 us
  transfers between devices with their start and end apart: 5, of which 4 were waited for; matrix products, arithmetic and copies ran while one was open for 17% of the time, Pallas kernels for 0%

profile of v1, /device:TPU:0, one launch (start us, length us, event | category | flops | bytes accessed | tf_op | source)
XLA Modules:
  0.0 404.9 jit_solution(9674740499030536314)
XLA Ops:
  6.5 0.0 all-gather.3.cloned.1.call-start
  6.5 0.7 all-gather.3.cloned.1.call-update
  7.3 0.0 all-gather.5.cloned.1.call-start
  7.3 0.7 all-gather.5.cloned.1.call-update
  8.0 161.8 %all-gather.3.cloned.1.call-done = f32[12288,512]{1,0:T(8,128)} async-done(((f32[12288,128]{1,0:T(8,128)}), f32[12288,512]{1,0:T(8,128)}) %all-gather.3.cloned.1.call-update) | async-done | bytes 25165840 | tf_op jit(solution)/shard_map/all_gather | solution.py:12
  169.8 44.3 %fusion.1 = f32[512,512]{1,0:T(8,128)S(1)} fusion(f32[12288,512]{1,0:T(8,128)} %all-gather.3.cloned.1.call-done, f32[12288,512]{1,0:T(8,128)} %param.6), kind=kOutput, calls=%fused_computation.2 | convolution fusion | flops 38654705664 | bytes 51380224 | tf_op jit(solution)/shard_map/dot_general | solution.py:13
  214.1 1.5 collective-permute-start
  215.6 23.8 %collective-permute-done = f32[512,512]{1,0:T(8,128)S(1)} collective-permute-done((f32[512,512]{1,0:T(8,128)S(1)}, f32[512,512]{1,0:T(8,128)S(1)}, u32[]{:S(2)}, u32[]{:S(2)}) %collective-permute-start) | collective-permute-done | bytes 1048608 | tf_op jit(solution)/shard_map/ppermute | solution.py:19
  239.5 0.2 add.12
  239.7 1.6 collective-permute-start.1
  241.2 23.1 %collective-permute-done.1 = f32[512,512]{1,0:T(8,128)S(1)} collective-permute-done((f32[512,512]{1,0:T(8,128)S(1)}, f32[512,512]{1,0:T(8,128)S(1)}, u32[]{:S(2)}, u32[]{:S(2)}) %collective-permute-start.1) | collective-permute-done | bytes 1048608 | tf_op jit(solution)/shard_map/ppermute | solution.py:19
  264.3 0.2 add.13
  264.5 2.5 collective-permute-start.2
  267.0 24.7 %copy.5 = f32[12288,512]{0,1:T(8,128)} copy(f32[12288,512]{1,0:T(8,128)} %param.7) | data formatting | bytes 50331648 | tf_op args[3]
  291.7 34.5 %all-gather.5.cloned.1.call-done = f32[512,12288]{1,0:T(8,128)} async-done(((f32[128,12288]{1,0:T(8,128)}), f32[512,12288]{1,0:T(8,128)}) %all-gather.5.cloned.1.call-update) | async-done | bytes 25165840 | tf_op jit(solution)/shard_map/all_gather | solution.py:8
  326.2 0.0 collective-permute-done.2
  326.2 47.2 %bitcast_add_fusion = f32[12288,512]{0,1:T(8,128)} fusion(f32[12288,512]{0,1:T(8,128)} %copy.5, f32[512,12288]{1,0:T(8,128)} %all-gather.5.cloned.1.call-done, f32[512,512]{1,0:T(8,128)S(1)} %add.13, f32[512,512]{1,0:T(8,128)S(1)} %collective-permute-done.2), kind=kOutput, calls=%fused_computation | convolution fusion | flops 38661259264 | bytes 77594624 | tf_op jit(solution)/shard_map/dot_general | solution.py:23
  373.4 24.7 %copy.6 = f32[12288,512]{1,0:T(8,128)} copy(f32[12288,512]{0,1:T(8,128)} %bitcast_add_fusion) | data formatting | bytes 50331648 | tf_op jit(solution)/shard_map/add | solution.py:23
Async XLA Ops:
  6.5 163.3 %all-gather.3.cloned.1.call-start = ((), (), s32[]{:S(2)}) async-start(), calls=%async_computation | async-start | bytes 31457280 | tf_op jit(solution)/shard_map/all_gather | solution.py:12
  7.3 318.9 %all-gather.5.cloned.1.call-start = ((), (), s32[]{:S(2)}) async-start(), calls=%async_computation.1 | async-start | bytes 31457280 | tf_op jit(solution)/shard_map/all_gather | solution.py:8
  214.1 25.4 %collective-permute-start = (f32[512,512]{1,0:T(8,128)S(1)}, f32[512,512]{1,0:T(8,128)S(1)}, u32[]{:S(2)}, u32[]{:S(2)}) collective-permute-start(f32[512,512]{1,0:T(8,128)S(1)} %fusion.1), channel_id=1, source_target_pairs={{0,4},{4,0},{8,12},{12,8},{16,20},{20,16},{24,28},{28,24},{1,5},{5... | collective-permute-start | bytes 3145736 | tf_op jit(solution)/shard_map/ppermute | solution.py:19
  239.7 24.6 %collective-permute-start.1 = (f32[512,512]{1,0:T(8,128)S(1)}, f32[512,512]{1,0:T(8,128)S(1)}, u32[]{:S(2)}, u32[]{:S(2)}) collective-permute-start(f32[512,512]{1,0:T(8,128)S(1)} %add.12), channel_id=1, source_target_pairs={{0,8},{4,12},{8,0},{12,4},{16,24},{20,28},{24,16},{28,20},{1,9},{5... | collective-permute-start | bytes 3145736 | tf_op jit(solution)/shard_map/ppermute | solution.py:19
  264.5 61.7 %collective-permute-start.2 = (f32[512,512]{1,0:T(8,128)S(1)}, f32[512,512]{1,0:T(8,128)S(1)}, u32[]{:S(2)}, u32[]{:S(2)}) collective-permute-start(f32[512,512]{1,0:T(8,128)S(1)} %add.13), channel_id=1, source_target_pairs={{0,16},{4,20},{8,24},{12,28},{16,0},{20,4},{24,8},{28,12},{1,17},{... | collective-permute-start | bytes 3145736 | tf_op jit(solution)/shard_map/ppermute | solution.py:19
Sparse Core Ops, SparseCore 0:
  8.9 160.8 all-gather.2
  171.4 154.7 all-gather.4
